TPU v7x, 128 devices: a whole 4x4x4 slice. The times are simulated.
128 devices in a mesh: pair: 8 (over x, core), ints: 16 (over y, z).
Axes of the slice: x: 4, y: 4, z: 4, core: 2. Of those that a mesh axis runs over, the one named last changes fastest.
Arguments:
- t2: bfloat16 [4096, 8192], P('pair', 'ints'), may hold values from -6 to 6
- t2_live: int32 [8, 64], P('pair', 'ints'), may hold values 0 or 1
- int_tiles: int32 [5120, 2], P('ints'), may hold values from 0 to 63
- integrals: bfloat16 [5120, 128, 128], P('ints'), may hold values from -0.0625 to 0.0625
- cycle_w: bfloat16 [4096, 4096], P('pair'), may hold values from -0.09375 to 0.09375
- res_live: int32 [8, 64], P('pair', 'ints'), may hold values 0 or 1
Outputs:
- residual: float32 [4096, 8192], P('pair', 'ints')
All inputs are finite; a program needn't handle non-finite values. No bound on the sum of `t2_live` or of `res_live` on one device may be relied on, other than what follows from the above.
Results may differ from a plain program's by a relative error of at most 0.0003.
Values may be sent and summed in bfloat16 or wider, within the bound.
No kernel may reach another device: no remote copies, remote signals or barrier semaphores. Data moves between devices by JAX's collectives and lax.ppermute only.
A program may use at most 192 MiB of HBM per device.

v0:
```python
import jax
import jax.numpy as jnp
from jax import lax
from jax.sharding import PartitionSpec as P


def local(t2, t2_live, int_tiles, integrals, cycle_w, res_live):
    rows_here = t2.shape[0]
    tile_size = integrals.shape[1]
    tiles_here = t2.shape[1] // tile_size
    live_mask = t2_live[0].astype(t2.dtype)
    amps = (t2.reshape(rows_here, tiles_here, tile_size) * live_mask[None, :, None]).reshape(
        rows_here, tiles_here * tile_size
    )
    block_amps = lax.all_gather(amps, "ints", axis=1, tiled=True)
    tiles_all = block_amps.shape[1] // tile_size
    amps_tiled = block_amps.reshape(rows_here, tiles_all, tile_size)
    count_here = integrals.shape[0]
    group_size = 64
    tile_groups = int_tiles.reshape(count_here // group_size, group_size, 2)
    int_groups = integrals.reshape(count_here // group_size, group_size, tile_size, tile_size)
    tile_ids = jnp.arange(tiles_all, dtype=jnp.int32)

    def ladder_step(partial_value, entry):
        pairs_uv, blocks = entry
        source_table = (pairs_uv[:, 0:1] == tile_ids[None, :]).astype(jnp.bfloat16)
        target_table = (pairs_uv[:, 1:2] == tile_ids[None, :]).astype(jnp.float32)
        picked = jnp.einsum(
            "jt,ptc->jpc", source_table, amps_tiled, preferred_element_type=jnp.float32
        ).astype(jnp.bfloat16)
        product = jnp.einsum("jpc,jcd->jpd", picked, blocks, preferred_element_type=jnp.float32)
        partial_value = partial_value + jnp.einsum(
            "jv,jpd->vpd", target_table, product, precision=lax.Precision.HIGHEST
        )
        return (partial_value, None)

    start_sum = jnp.zeros((tiles_all, rows_here, tile_size), jnp.float32)
    partial_value, _ = lax.scan(ladder_step, start_sum, (tile_groups, int_groups))
    summed = lax.psum(partial_value, "ints")
    owned = lax.dynamic_slice_in_dim(summed, lax.axis_index("ints") * tiles_here, tiles_here, 0)
    ladder = owned.transpose(1, 0, 2).reshape(rows_here, tiles_here * tile_size)
    cycle_term = jnp.dot(
        cycle_w,
        lax.all_gather(amps, "pair", axis=0, tiled=True),
        preferred_element_type=jnp.float32,
    )
    keep_mask = jnp.repeat(res_live[0], tile_size).astype(jnp.float32)[None, :]
    return keep_mask * (ladder + cycle_term)


def solution(mesh):
    placed = (
        P("pair", "ints"),
        P("pair", "ints"),
        P("ints", None),
        P("ints", None, None),
        P("pair", None),
        P("pair", "ints"),
    )
    return jax.shard_map(
        local, mesh=mesh, in_specs=placed, out_specs=P("pair", "ints"), check_vma=False
    )
```

profile of v0, /device:TPU:1, one launch (start us, length us, event | category | flops | bytes accessed | tf_op | source)
XLA Modules:
  0.0 551.5 jit_solution(12331240370962497261)
XLA Ops:
  8.1 1.9 broadcast_multiply_fusion
  10.1 0.8 reshape.30
  10.8 80.4 %all-gather.3.cloned.1.call-done = bf16[512,8192]{1,0:T(8,128)(2,1)} async-done(((bf16[512,512]{1,0:T(8,128)(2,1)}), bf16[512,8192]{1,0:T(8,128)(2,1)}) %all-gather.3.cloned.1.call-update) | async-done | bytes 8388624 | tf_op jit(solution)/shard_map/all_gather | solution.py:15
  91.2 9.3 %copy.15 = bf16[64,8,64,128]{3,2,1,0:T(8,128)(2,1)} copy(bf16[64,8,64,128]{3,1,2,0:T(8,128)(2,1)} %bitcast.55) | data formatting | bytes 16777216
  100.5 213.6 %while.12 = (s32[]{:T(128)}, f32[64,512,128]{2,0,1:T(8,128)}, s32[5,64,2]{1,0,2:T(8,128)S(1)}, bf16[512,64,128]{2,1,0:T(8,128)(2,1)}, bf16[5,64,128,128]{3,2,1,0:T(8,128)(2,1)}, /*index=5*/s32[]{:T(128)}, s32[]{:T(128)}) while((s32[]{:T(128)}, f32[64,512,128]{2,0,1:T(8,128)}, s32[5,64,2]{1,0,2:T(8,128)S(1)}, ...), condition=%wide.region_1.2_spmd.clone.clone, body=%wide.region_0.1_spmd.clone.clone.sunk | while | flops 4840235008 | bytes 94374496 | solution.py:38
  100.5 5.8 %fusion.34 = bf16[64,512,128]{2,0,1:T(8,128)(2,1)S(1)} fusion(bf16[512,64,128]{2,1,0:T(8,128)(2,1)} %get-tuple-element.146, s32[64]{0:T(128)S(1)} %get-tuple-element.127), kind=kOutput, calls=%fused_computation.12.clone.1 | convolution fusion | flops 536875008 | bytes 16777472 | tf_op jit(solution)/shard_map/while/body/eval_jaxpr/jt,ptc->jpc/dot_general | solution.py:28
  106.3 13.9 %fusion.35 = f32[64,512,128]{2,1,0:T(8,128)} fusion(bf16[64,512,128]{2,0,1:T(8,128)(2,1)S(1)} %fusion.34, bf16[5,64,128,128]{3,2,1,0:T(8,128)(2,1)} %get-tuple-element.147, s32[]{:T(128)S(6)} %copy.28), kind=kOutput, calls=%fused_computation.5.clone.1 | convolution fusion | flops 1073741824 | bytes 27262980 | tf_op jit(solution)/shard_map/while/body/eval_jaxpr/jpc,jcd->jpd/dot_general | solution.py:31
  120.2 20.4 %select_add_fusion.2 = f32[64,512,128]{2,0,1:T(8,128)} fusion(f32[64,512,128]{2,0,1:T(8,128)} %get-tuple-element.137, f32[64,512,128]{2,1,0:T(8,128)} %fusion.35, pred[]{:T(512)S(6)} %compare.3, s32[64]{0:T(128)S(1)} %get-tuple-element.128), kind=kOutput, calls=%fused_computation.4.clone.1 | convolution fusion | flops 3229618176 | bytes 50331904 | tf_op jit(solution)/shard_map/while/body/eval_jaxpr/jv,jpd->vpd/dot_general | solution.py:32
  140.6 5.8 %fusion.34 = bf16[64,512,128]{2,0,1:T(8,128)(2,1)S(1)} fusion(bf16[512,64,128]{2,1,0:T(8,128)(2,1)} %get-tuple-element.146, s32[64]{0:T(128)S(1)} %get-tuple-element.127), kind=kOutput, calls=%fused_computation.12.clone.1 | convolution fusion | flops 536875008 | bytes 16777472 | tf_op jit(solution)/shard_map/while/body/eval_jaxpr/jt,ptc->jpc/dot_general | solution.py:28
  146.4 13.9 %fusion.35 = f32[64,512,128]{2,1,0:T(8,128)} fusion(bf16[64,512,128]{2,0,1:T(8,128)(2,1)S(1)} %fusion.34, bf16[5,64,128,128]{3,2,1,0:T(8,128)(2,1)} %get-tuple-element.147, s32[]{:T(128)S(6)} %copy.28), kind=kOutput, calls=%fused_computation.5.clone.1 | convolution fusion | flops 1073741824 | bytes 27262980 | tf_op jit(solution)/shard_map/while/body/eval_jaxpr/jpc,jcd->jpd/dot_general | solution.py:31
  160.3 23.7 %select_add_fusion.2 = f32[64,512,128]{2,0,1:T(8,128)} fusion(f32[64,512,128]{2,0,1:T(8,128)} %get-tuple-element.137, f32[64,512,128]{2,1,0:T(8,128)} %fusion.35, pred[]{:T(512)S(6)} %compare.3, s32[64]{0:T(128)S(1)} %get-tuple-element.128), kind=kOutput, calls=%fused_computation.4.clone.1 | convolution fusion | flops 3229618176 | bytes 50331904 | tf_op jit(solution)/shard_map/while/body/eval_jaxpr/jv,jpd->vpd/dot_general | solution.py:32
  184.0 5.8 %fusion.34 = bf16[64,512,128]{2,0,1:T(8,128)(2,1)S(1)} fusion(bf16[512,64,128]{2,1,0:T(8,128)(2,1)} %get-tuple-element.146, s32[64]{0:T(128)S(1)} %get-tuple-element.127), kind=kOutput, calls=%fused_computation.12.clone.1 | convolution fusion | flops 536875008 | bytes 16777472 | tf_op jit(solution)/shard_map/while/body/eval_jaxpr/jt,ptc->jpc/dot_general | solution.py:28
  189.8 13.9 %fusion.35 = f32[64,512,128]{2,1,0:T(8,128)} fusion(bf16[64,512,128]{2,0,1:T(8,128)(2,1)S(1)} %fusion.34, bf16[5,64,128,128]{3,2,1,0:T(8,128)(2,1)} %get-tuple-element.147, s32[]{:T(128)S(6)} %copy.28), kind=kOutput, calls=%fused_computation.5.clone.1 | convolution fusion | flops 1073741824 | bytes 27262980 | tf_op jit(solution)/shard_map/while/body/eval_jaxpr/jpc,jcd->jpd/dot_general | solution.py:31
  203.7 23.7 %select_add_fusion.2 = f32[64,512,128]{2,0,1:T(8,128)} fusion(f32[64,512,128]{2,0,1:T(8,128)} %get-tuple-element.137, f32[64,512,128]{2,1,0:T(8,128)} %fusion.35, pred[]{:T(512)S(6)} %compare.3, s32[64]{0:T(128)S(1)} %get-tuple-element.128), kind=kOutput, calls=%fused_computation.4.clone.1 | convolution fusion | flops 3229618176 | bytes 50331904 | tf_op jit(solution)/shard_map/while/body/eval_jaxpr/jv,jpd->vpd/dot_general | solution.py:32
  227.4 5.8 %fusion.34 = bf16[64,512,128]{2,0,1:T(8,128)(2,1)S(1)} fusion(bf16[512,64,128]{2,1,0:T(8,128)(2,1)} %get-tuple-element.146, s32[64]{0:T(128)S(1)} %get-tuple-element.127), kind=kOutput, calls=%fused_computation.12.clone.1 | convolution fusion | flops 536875008 | bytes 16777472 | tf_op jit(solution)/shard_map/while/body/eval_jaxpr/jt,ptc->jpc/dot_general | solution.py:28
  233.1 13.9 %fusion.35 = f32[64,512,128]{2,1,0:T(8,128)} fusion(bf16[64,512,128]{2,0,1:T(8,128)(2,1)S(1)} %fusion.34, bf16[5,64,128,128]{3,2,1,0:T(8,128)(2,1)} %get-tuple-element.147, s32[]{:T(128)S(6)} %copy.28), kind=kOutput, calls=%fused_computation.5.clone.1 | convolution fusion | flops 1073741824 | bytes 27262980 | tf_op jit(solution)/shard_map/while/body/eval_jaxpr/jpc,jcd->jpd/dot_general | solution.py:31
  247.1 23.7 %select_add_fusion.2 = f32[64,512,128]{2,0,1:T(8,128)} fusion(f32[64,512,128]{2,0,1:T(8,128)} %get-tuple-element.137, f32[64,512,128]{2,1,0:T(8,128)} %fusion.35, pred[]{:T(512)S(6)} %compare.3, s32[64]{0:T(128)S(1)} %get-tuple-element.128), kind=kOutput, calls=%fused_computation.4.clone.1 | convolution fusion | flops 3229618176 | bytes 50331904 | tf_op jit(solution)/shard_map/while/body/eval_jaxpr/jv,jpd->vpd/dot_general | solution.py:32
  270.7 5.8 %fusion.34 = bf16[64,512,128]{2,0,1:T(8,128)(2,1)S(1)} fusion(bf16[512,64,128]{2,1,0:T(8,128)(2,1)} %get-tuple-element.146, s32[64]{0:T(128)S(1)} %get-tuple-element.127), kind=kOutput, calls=%fused_computation.12.clone.1 | convolution fusion | flops 536875008 | bytes 16777472 | tf_op jit(solution)/shard_map/while/body/eval_jaxpr/jt,ptc->jpc/dot_general | solution.py:28
  276.5 13.9 %fusion.35 = f32[64,512,128]{2,1,0:T(8,128)} fusion(bf16[64,512,128]{2,0,1:T(8,128)(2,1)S(1)} %fusion.34, bf16[5,64,128,128]{3,2,1,0:T(8,128)(2,1)} %get-tuple-element.147, s32[]{:T(128)S(6)} %copy.28), kind=kOutput, calls=%fused_computation.5.clone.1 | convolution fusion | flops 1073741824 | bytes 27262980 | tf_op jit(solution)/shard_map/while/body/eval_jaxpr/jpc,jcd->jpd/dot_general | solution.py:31
  290.4 23.7 %select_add_fusion.2 = f32[64,512,128]{2,0,1:T(8,128)} fusion(f32[64,512,128]{2,0,1:T(8,128)} %get-tuple-element.137, f32[64,512,128]{2,1,0:T(8,128)} %fusion.35, pred[]{:T(512)S(6)} %compare.3, s32[64]{0:T(128)S(1)} %get-tuple-element.128), kind=kOutput, calls=%fused_computation.4.clone.1 | convolution fusion | flops 3229618176 | bytes 50331904 | tf_op jit(solution)/shard_map/while/body/eval_jaxpr/jv,jpd->vpd/dot_general | solution.py:32
  314.8 219.9 %all-reduce.2.cloned.1.call-done = f32[64,512,128]{2,0,1:T(8,128)} async-done(((f32[64,512,128]{2,0,1:T(8,128)}), f32[64,512,128]{2,0,1:T(8,128)}) %all-reduce.2.cloned.1.call-update) | async-done | bytes 16777232 | tf_op jit(solution)/shard_map/psum | solution.py:39
  534.7 1.8 dynamic-slice_bitcast_fusion
  536.9 5.8 %fusion.18 = f32[512,512]{0,1:T(8,128)S(1)} fusion(f32[512,512]{0,1:T(8,128)S(1)} %bitcast.56, bf16[4096,512]{1,0:T(8,128)(2,1)} %all-gather.5.cloned.1.call-done, bf16[512,4096]{1,0:T(8,128)(2,1)} %param.12, f32[512]{0:T(512)S(1)} %broadcast_bitcast_fusion), kind=kOutput, calls=%fused_computation.21 | convolution fusion | flops 2148007936 | bytes 10487808 | tf_op jit(solution)/shard_map/dot_general | solution.py:42
  542.8 1.3 copy.11
  (25 shorter events, 1.9 us)
Async XLA Ops:
  7.4 83.8 %all-gather.3.cloned.1.call-start = ((), (), s32[]{:S(2)}) async-start(), calls=%async_computation | async-start | bytes 8912896 | tf_op jit(solution)/shard_map/all_gather | solution.py:15
  10.0 524.7 %all-reduce.2.cloned.1.call-start = ((), (), s32[]{:S(2)}) async-start(), calls=%async_computation.1 | async-start | bytes 33554432 | tf_op jit(solution)/shard_map/psum | solution.py:39
  314.1 0.7 copy-start
  314.1 222.8 %all-gather.5.cloned.1.call-start = ((), (), s32[]{:S(2)}) async-start(), calls=%async_computation.2 | async-start | bytes 4718592 | tf_op jit(solution)/shard_map/all_gather | solution.py:44
Sparse Core Ops, SparseCore 0:
  10.3 80.8 all-gather.2
  314.2 220.4 all-reduce.1
Sparse Core Ops, SparseCore 1:
  316.3 32.4 all-gather.4
where the time goes:
time: 552 us
  waiting for transfers between devices  301 us (55%)
  matrix products  219 us (40%)
  between operations  14.9 us (3%)
  local copies, waits for them, and re-layouts  13.7 us (2%)
    psum x1, waiting for transfers between devices, local(): summed = lax.psum(partial_value, 'ints')  220 us
    dot_general x5, matrix products, ladder_step(): jnp.einsum('jv,jpd->vpd', target_table, product, precision=lax.Precision....  115 us
    all_gather x1, waiting for transfers between devices, local(): block_amps = lax.all_gather(amps, 'ints', axis=1, tiled=True)  80.4 us
    dot_general x5, matrix products, ladder_step(): jnp.einsum('jpc,jcd->jpd', picked, blocks, preferred_element_type=jnp.flo...  69.7 us
    dot_general x5, matrix products, ladder_step(): jnp.einsum('jt,ptc->jpc', source_table, amps_tiled, preferred_element_typ...  28.8 us
  transfers between devices with their start and end apart: 3, of which 2 were waited for; matrix products, arithmetic and copies ran while one was open for 1% of the time, Pallas kernels for 0%

commit v1 on v0

--- a/solution.py
+++ b/solution.py
@@ -36,7 +36,10 @@
 
     start_sum = jnp.zeros((tiles_all, rows_here, tile_size), jnp.float32)
     partial_value, _ = lax.scan(ladder_step, start_sum, (tile_groups, int_groups))
-    summed = lax.psum(partial_value, "ints")
+    peers, summed = (lax.axis_size("ints"), partial_value)
+    for far in [1 << k for k in range(peers.bit_length() - 1)]:
+        swap = [(i, i ^ far) for i in range(peers)]
+        summed = summed + lax.ppermute(summed, "ints", swap)
     owned = lax.dynamic_slice_in_dim(summed, lax.axis_index("ints") * tiles_here, tiles_here, 0)
     ladder = owned.transpose(1, 0, 2).reshape(rows_here, tiles_here * tile_size)
     cycle_term = jnp.dot(

time: 552 us -> 1810 us (3.28)
  waiting for transfers between devices: 301 us -> 1510 us
  other arithmetic: 2.53 us -> 41.7 us
    ppermute x0 -> x4, waiting for transfers between devices: none -> 1430 us  [local(): summed = summed + lax.ppermute(summed, 'ints', swap)]
    psum x1 -> x0, waiting for transfers between devices: 220 us -> none  [local(): summed = lax.psum(partial_value, 'ints')]
    add x0 -> x3, other arithmetic: none -> 36.6 us  [local(): summed = summed + lax.ppermute(summed, 'ints', swap)]
  transfers between devices with their start and end apart: 3 -> 6, of which waited for: 2 -> 5; matrix products, arithmetic and copies ran while one was open for 1% -> 0% of each run, Pallas kernels for 0% -> 0%
where the time goes in v1:
time: 1810 us
  waiting for transfers between devices  1510 us (83%)
  matrix products  220 us (12%)
  other arithmetic  41.7 us (2%)
    ppermute x4, waiting for transfers between devices, local(): summed = summed + lax.ppermute(summed, 'ints', swap)  1430 us
    dot_general x5, matrix products, ladder_step(): jnp.einsum('jv,jpd->vpd', target_table, product, precision=lax.Precision....  115 us
    all_gather x1, waiting for transfers between devices, local(): block_amps = lax.all_gather(amps, 'ints', axis=1, tiled=True)  80.4 us
    dot_general x5, matrix products, ladder_step(): jnp.einsum('jpc,jcd->jpd', picked, blocks, preferred_element_type=jnp.flo...  69.9 us
    add x3, other arithmetic, local(): summed = summed + lax.ppermute(summed, 'ints', swap)  36.6 us
  transfers between devices with their start and end apart: 6, of which 5 were waited for; matrix products, arithmetic and copies ran while one was open for 0% of the time, Pallas kernels for 0%

profile of v1, /device:TPU:1, one launch (start us, length us, event | category | flops | bytes accessed | tf_op | source)
XLA Modules:
  0.0 1807.8 jit_solution(11148708350231874698)
XLA Ops:
  10.8 80.4 %all-gather.3.cloned.1.call-done = bf16[512,8192]{1,0:T(8,128)(2,1)} async-done(((bf16[512,512]{1,0:T(8,128)(2,1)}), bf16[512,8192]{1,0:T(8,128)(2,1)}) %all-gather.3.cloned.1.call-update) | async-done | bytes 8388624 | tf_op jit(solution)/shard_map/all_gather | solution.py:15
  91.2 9.3 copy.15
  100.5 213.9 %while.12 = (s32[]{:T(128)}, f32[64,512,128]{2,0,1:T(8,128)}, s32[5,64,2]{1,0,2:T(8,128)S(1)}, bf16[512,64,128]{2,1,0:T(8,128)(2,1)}, bf16[5,64,128,128]{3,2,1,0:T(8,128)(2,1)}, /*index=5*/s32[]{:T(128)}, s32[]{:T(128)}) while((s32[]{:T(128)}, f32[64,512,128]{2,0,1:T(8,128)}, s32[5,64,2]{1,0,2:T(8,128)S(1)}, ...), condition=%wide.region_1.2_spmd.clone.clone, body=%wide.region_0.1_spmd.clone.clone.sunk | while | flops 4840235008 | bytes 94375000 | solution.py:38
  106.3 14.0 fusion.35
  120.3 20.4 %select_add_fusion.2 = f32[64,512,128]{2,0,1:T(8,128)} fusion(f32[64,512,128]{2,0,1:T(8,128)} %get-tuple-element.137, f32[64,512,128]{2,1,0:T(8,128)} %fusion.35, pred[]{:T(512)S(6)} %compare.3, s32[64]{0:T(128)S(1)} %get-tuple-element.128), kind=kOutput, calls=%fused_computation.4.clone.1 | convolution fusion | flops 3229618176 | bytes 50331904 | tf_op jit(solution)/shard_map/while/body/eval_jaxpr/jv,jpd->vpd/dot_general | solution.py:32
  140.7 5.8 fusion.34
  146.5 14.0 fusion.35
  160.5 23.7 %select_add_fusion.2 = f32[64,512,128]{2,0,1:T(8,128)} fusion(f32[64,512,128]{2,0,1:T(8,128)} %get-tuple-element.137, f32[64,512,128]{2,1,0:T(8,128)} %fusion.35, pred[]{:T(512)S(6)} %compare.3, s32[64]{0:T(128)S(1)} %get-tuple-element.128), kind=kOutput, calls=%fused_computation.4.clone.1 | convolution fusion | flops 3229618176 | bytes 50331904 | tf_op jit(solution)/shard_map/while/body/eval_jaxpr/jv,jpd->vpd/dot_general | solution.py:32
  184.1 5.8 fusion.34
  189.9 14.0 fusion.35
  203.9 23.7 %select_add_fusion.2 = f32[64,512,128]{2,0,1:T(8,128)} fusion(f32[64,512,128]{2,0,1:T(8,128)} %get-tuple-element.137, f32[64,512,128]{2,1,0:T(8,128)} %fusion.35, pred[]{:T(512)S(6)} %compare.3, s32[64]{0:T(128)S(1)} %get-tuple-element.128), kind=kOutput, calls=%fused_computation.4.clone.1 | convolution fusion | flops 3229618176 | bytes 50331904 | tf_op jit(solution)/shard_map/while/body/eval_jaxpr/jv,jpd->vpd/dot_general | solution.py:32
  233.3 14.0 fusion.35
  247.3 23.7 %select_add_fusion.2 = f32[64,512,128]{2,0,1:T(8,128)} fusion(f32[64,512,128]{2,0,1:T(8,128)} %get-tuple-element.137, f32[64,512,128]{2,1,0:T(8,128)} %fusion.35, pred[]{:T(512)S(6)} %compare.3, s32[64]{0:T(128)S(1)} %get-tuple-element.128), kind=kOutput, calls=%fused_computation.4.clone.1 | convolution fusion | flops 3229618176 | bytes 50331904 | tf_op jit(solution)/shard_map/while/body/eval_jaxpr/jv,jpd->vpd/dot_general | solution.py:32
  271.0 5.8 fusion.34
  276.8 14.0 fusion.35
  290.7 23.7 %select_add_fusion.2 = f32[64,512,128]{2,0,1:T(8,128)} fusion(f32[64,512,128]{2,0,1:T(8,128)} %get-tuple-element.137, f32[64,512,128]{2,1,0:T(8,128)} %fusion.35, pred[]{:T(512)S(6)} %compare.3, s32[64]{0:T(128)S(1)} %get-tuple-element.128), kind=kOutput, calls=%fused_computation.4.clone.1 | convolution fusion | flops 3229618176 | bytes 50331904 | tf_op jit(solution)/shard_map/while/body/eval_jaxpr/jv,jpd->vpd/dot_general | solution.py:32
  315.3 359.6 %collective-permute-done = f32[64,512,128]{2,0,1:T(8,128)} collective-permute-done((f32[64,512,128]{2,0,1:T(8,128)}, f32[64,512,128]{2,0,1:T(8,128)}, u32[]{:S(2)}, u32[]{:S(2)}) %collective-permute-start) | collective-permute-done | bytes 16777248 | tf_op jit(solution)/shard_map/ppermute | solution.py:42
  674.9 11.8 add.24
  688.9 358.7 %collective-permute-done.1 = f32[64,512,128]{2,0,1:T(8,128)} collective-permute-done((f32[64,512,128]{2,0,1:T(8,128)S(1)}, f32[64,512,128]{2,0,1:T(8,128)}, u32[]{:S(2)}, u32[]{:S(2)}) %collective-permute-start.1) | collective-permute-done | bytes 16777248 | tf_op jit(solution)/shard_map/ppermute | solution.py:42
  1047.6 12.4 add.25
  1061.0 357.6 %collective-permute-done.2 = f32[64,512,128]{2,0,1:T(8,128)S(1)} collective-permute-done((f32[64,512,128]{2,0,1:T(8,128)}, f32[64,512,128]{2,0,1:T(8,128)S(1)}, u32[]{:S(2)}, u32[]{:S(2)}) %collective-permute-start.2) | collective-permute-done | bytes 16777248 | tf_op jit(solution)/shard_map/ppermute | solution.py:42
  1418.6 12.4 add.26
  1433.3 357.0 %collective-permute-done.3 = f32[64,512,128]{2,0,1:T(8,128)} collective-permute-done((f32[64,512,128]{2,0,1:T(8,128)}, f32[64,512,128]{2,0,1:T(8,128)}, u32[]{:S(2)}, u32[]{:S(2)}) %collective-permute-start.3) | collective-permute-done | bytes 16777248 | tf_op jit(solution)/shard_map/ppermute | solution.py:42
  1793.2 5.8 fusion.18
  (33 shorter events, 25.5 us)
Async XLA Ops:
  7.4 83.8 %all-gather.3.cloned.1.call-start = ((), (), s32[]{:S(2)}) async-start(), calls=%async_computation | async-start | bytes 8912896 | tf_op jit(solution)/shard_map/all_gather | solution.py:15
  10.0 1783.2 %all-gather.5.cloned.1.call-start = ((), (), s32[]{:S(2)}) async-start(), calls=%async_computation.1 | async-start | bytes 4718592 | tf_op jit(solution)/shard_map/all_gather | solution.py:47
  314.4 360.5 %collective-permute-start = (f32[64,512,128]{2,0,1:T(8,128)}, f32[64,512,128]{2,0,1:T(8,128)}, u32[]{:S(2)}, u32[]{:S(2)}) collective-permute-start(f32[64,512,128]{2,0,1:T(8,128)} %get-tuple-element.40), channel_id=1, source_target_pairs={{0,1},{1,0},{2,3},{3,2},{4,5},{5,4},{6,7},{7,6},{8,9},{9,8},{10,11... | collective-permute-start | bytes 50331656 | tf_op jit(solution)/shard_map/ppermute | solution.py:42
  686.7 360.9 %collective-permute-start.1 = (f32[64,512,128]{2,0,1:T(8,128)S(1)}, f32[64,512,128]{2,0,1:T(8,128)}, u32[]{:S(2)}, u32[]{:S(2)}) collective-permute-start(f32[64,512,128]{2,0,1:T(8,128)S(1)} %add.24), channel_id=1, source_target_pairs={{0,2},{1,3},{2,0},{3,1},{4,6},{5,7},{6,4},{7,5},{8,10},{9,11},{10,... | collective-permute-start | bytes 50331656 | tf_op jit(solution)/shard_map/ppermute | solution.py:42
  1060.1 373.1 %copy-start = (s32[1,4]{1,0:T(1,128)S(1)}, s32[1,4]{1,0:T(1,128)}, u32[]{:S(2)}) copy-start(s32[1,4]{1,0:T(1,128)} %param.13) | copy-start | bytes 52
  1060.1 358.5 %collective-permute-start.2 = (f32[64,512,128]{2,0,1:T(8,128)}, f32[64,512,128]{2,0,1:T(8,128)S(1)}, u32[]{:S(2)}, u32[]{:S(2)}) collective-permute-start(f32[64,512,128]{2,0,1:T(8,128)} %add.25), channel_id=1, source_target_pairs={{0,4},{1,5},{2,6},{3,7},{4,0},{5,1},{6,2},{7,3},{8,12},{9,13},{10,... | collective-permute-start | bytes 50331656 | tf_op jit(solution)/shard_map/ppermute | solution.py:42
  1431.0 359.2 %collective-permute-start.3 = (f32[64,512,128]{2,0,1:T(8,128)}, f32[64,512,128]{2,0,1:T(8,128)}, u32[]{:S(2)}, u32[]{:S(2)}) collective-permute-start(f32[64,512,128]{2,0,1:T(8,128)} %add.26), channel_id=1, source_target_pairs={{0,8},{1,9},{2,10},{3,11},{4,12},{5,13},{6,14},{7,15},{8,0},{9,1},... | collective-permute-start | bytes 50331656 | tf_op jit(solution)/shard_map/ppermute | solution.py:42
Sparse Core Ops, SparseCore 0:
  10.3 80.8 all-gather.2
Sparse Core Ops, SparseCore 1:
  1433.3 35.1 all-gather.4
